TPU v7x, 32 devices: a whole 2x2x4 slice. The times are simulated.
32 devices in a mesh: dp: 8 (over z, x), seq: 4 (over y, core).
Axes of the slice: x: 2, y: 2, z: 4, core: 2. Of those that a mesh axis runs over, the one named last changes fastest.
Arguments:
- tokens: bfloat16 [16, 1024, 1600], P('dp', 'seq'), may hold values from -6 to 6
- span_order: int32 [16, 8], P('dp'), may hold values from 0 to 7, each once within a row
- qkv_weight: bfloat16 [1600, 4800], P('seq', 'dp'), may hold values from -0.15625 to 0.15625
- out_weight: bfloat16 [1600, 1600], P('seq', 'dp'), may hold values from -0.625 to 0.625
- fc_weight: bfloat16 [1600, 6400], P('seq', 'dp'), may hold values from -0.15625 to 0.15625
- proj_weight: bfloat16 [6400, 1600], P('seq', 'dp'), may hold values from -0.078125 to 0.078125
- ln1_gain: bfloat16 [1600], P('seq'), may hold values from 0.5 to 1.5
- ln1_bias: bfloat16 [1600], P('seq'), may hold values from -1.75 to 1.75
- qv_bias: bfloat16 [2, 1600], P(None, 'seq'), may hold values from -1.75 to 1.75
- out_bias: bfloat16 [1600], P('seq'), may hold values from -1.75 to 1.75
- ln2_gain: bfloat16 [1600], P('seq'), may hold values from 0.5 to 1.5
- ln2_bias: bfloat16 [1600], P('seq'), may hold values from -1.75 to 1.75
- fc_bias: bfloat16 [6400], P('seq'), may hold values from -1.75 to 1.75
- proj_bias: bfloat16 [1600], P('seq'), may hold values from -1.75 to 1.75
- out_grad: bfloat16 [16, 1024, 1600], P('dp', 'seq'), may hold values from -6 to 6
Outputs:
- output: bfloat16 [16, 1024, 1600], P('dp', 'seq')
- input_grad: bfloat16 [16, 1024, 1600], P('dp', 'seq')
- qkv_weight_grad: float32 [1600, 4800], P('seq', 'dp')
- out_weight_grad: float32 [1600, 1600], P('seq', 'dp')
- fc_weight_grad: float32 [1600, 6400], P('seq', 'dp')
- proj_weight_grad: float32 [6400, 1600], P('seq', 'dp')
- ln1_gain_grad: float32 [1600], P('seq')
- ln1_bias_grad: float32 [1600], P('seq')
- qv_bias_grad: float32 [2, 1600], P(None, 'seq')
- out_bias_grad: float32 [1600], P('seq')
- ln2_gain_grad: float32 [1600], P('seq')
- ln2_bias_grad: float32 [1600], P('seq')
- fc_bias_grad: float32 [6400], P('seq')
- proj_bias_grad: float32 [1600], P('seq')
Inputs may be any that keep to these rules, and one draw needn't show every extreme that they name: `span_order`: each row is a permutation of the spans 0 to 7 of its sequence.
All inputs are finite; a program needn't handle non-finite values.
Results may differ from a plain program's by a relative error of at most 0.02.
Values may be sent and summed in bfloat16 or wider, within the bound.
A program may use at most 384 MiB of HBM per device.

v0:
```python
import jax
import jax.numpy as jnp
from jax import lax
from jax.sharding import PartitionSpec as P

HEAD = 64
MB_SEQS = 1


def layer_norm(value, gain, shift):
    center = jnp.mean(value, axis=-1, keepdims=True)
    offsets = value - center
    spread = jnp.mean(offsets * offsets, axis=-1, keepdims=True)
    return offsets * lax.rsqrt(spread + 1e-05) * gain + shift


def norm_grad(value, gain, shift, cotangent):
    result, pullback = jax.vjp(layer_norm, value, gain, shift)
    return pullback(cotangent)


def smooth_gate(value):
    return jax.nn.gelu(value, approximate=True)


def gate_grad(value, cotangent):
    result, pullback = jax.vjp(smooth_gate, value)
    return pullback(cotangent)[0]


def place_table(order, length, block):
    rows = jnp.arange(length, dtype=jnp.int32)
    span_ids = jnp.arange(order.shape[-1], dtype=jnp.int32)
    picks = (rows // block)[:, None] == span_ids[None, :]
    starts = jnp.sum(jnp.where(picks[None], order[:, None, :], 0), axis=-1)
    return starts * block + rows % block


def spread_product(left, columns):
    return jnp.dot(
        left, lax.all_gather(columns, "dp", axis=1, tiled=True), preferred_element_type=jnp.float32
    )


def back_product(grads, columns):
    return lax.dot_general(
        grads,
        lax.all_gather(columns, "dp", axis=1, tiled=True),
        (((1,), (1,)), ((), ())),
        preferred_element_type=jnp.float32,
    )


def masked_scores(queries, key_heads, query_places, key_places):
    scale = queries.shape[-1] ** (-0.5)
    scores = (
        jnp.einsum("qhd,khd->hqk", queries, key_heads, preferred_element_type=jnp.float32) * scale
    )
    allowed = key_places[None, :] <= query_places[:, None]
    return (jnp.where(allowed[None], scores, -1e30), allowed)


def attend(item):
    queries, key_rows, value_rows, query_places, key_places = item
    heads = queries.shape[1]
    key_heads = key_rows.reshape(key_rows.shape[0], heads, -1)
    value_heads = value_rows.reshape(value_rows.shape[0], heads, -1)
    scores, allowed = masked_scores(queries, key_heads, query_places, key_places)
    row_max = jnp.max(scores, axis=-1, keepdims=True)
    weights = jnp.exp(scores - row_max)
    row_total = jnp.sum(weights, axis=-1, keepdims=True)
    probs = (weights / row_total).astype(jnp.bfloat16)
    attended = jnp.einsum("hqk,khd->qhd", probs, value_heads, preferred_element_type=jnp.float32)
    return (attended, (row_max + jnp.log(row_total))[:, :, 0])


def attend_back(item):
    queries, key_rows, value_rows, query_places, key_places, log_total, grad_out = item
    heads = queries.shape[1]
    scale = queries.shape[-1] ** (-0.5)
    key_heads = key_rows.reshape(key_rows.shape[0], heads, -1)
    value_heads = value_rows.reshape(value_rows.shape[0], heads, -1)
    scores, allowed = masked_scores(queries, key_heads, query_places, key_places)
    probs = jnp.where(allowed[None], jnp.exp(scores - log_total[:, :, None]), 0.0)
    grad_probs = jnp.einsum(
        "qhd,khd->hqk", grad_out, value_heads, preferred_element_type=jnp.float32
    )
    centre = jnp.sum(probs * grad_probs, axis=-1, keepdims=True)
    grad_scores = (probs * (grad_probs - centre)).astype(jnp.bfloat16)
    grad_queries = (
        jnp.einsum("hqk,khd->qhd", grad_scores, key_heads, preferred_element_type=jnp.float32)
        * scale
    )
    grad_keys = (
        jnp.einsum("hqk,qhd->khd", grad_scores, queries, preferred_element_type=jnp.float32) * scale
    )
    grad_values = jnp.einsum(
        "hqk,qhd->khd", probs.astype(jnp.bfloat16), grad_out, preferred_element_type=jnp.float32
    )
    query_count = queries.shape[0]
    key_count = key_rows.shape[0]
    return (
        grad_queries.reshape(query_count, -1),
        grad_keys.reshape(key_count, -1),
        grad_values.reshape(key_count, -1),
    )


def local(
    tokens,
    span_order,
    qkv_weight,
    out_weight,
    fc_weight,
    proj_weight,
    ln1_gain,
    ln1_bias,
    qv_bias,
    out_bias,
    ln2_gain,
    ln2_bias,
    fc_bias,
    proj_bias,
    out_grad,
):
    seq_count = lax.axis_size("seq")
    dp_count = lax.axis_size("dp")
    local_len = tokens.shape[1]
    width = tokens.shape[2]
    full_len = local_len * seq_count
    block = full_len // span_order.shape[1]
    group = MB_SEQS
    rounds = tokens.shape[0] // group
    row_count = group * local_len
    heads = width // HEAD
    hidden_width = fc_weight.shape[1] * dp_count
    places = place_table(span_order, full_len, block)
    own_places = lax.dynamic_slice_in_dim(places, lax.axis_index("seq") * local_len, local_len, 1)
    local_weights = (qkv_weight, out_weight, fc_weight, proj_weight)
    weight_sums = [
        jnp.zeros((item.shape[0] * seq_count, item.shape[1] * dp_count), jnp.float32)
        for item in local_weights
    ]
    vector_shapes = (
        (width,),
        (width,),
        (2, width),
        (width,),
        (width,),
        (width,),
        (hidden_width,),
        (width,),
    )
    vector_sums = [jnp.zeros(shape, jnp.float32) for shape in vector_shapes]
    outputs = []
    input_grads = []
    for index in range(rounds):
        first = index * group
        batch_tokens = tokens[first : first + group]
        batch_grad = out_grad[first : first + group]
        batch_places = places[first : first + group]
        batch_own = own_places[first : first + group]
        gathered = (
            lax.all_gather(qkv_weight, "seq", axis=0, tiled=True),
            lax.all_gather(out_weight, "seq", axis=0, tiled=True),
            lax.all_gather(fc_weight, "seq", axis=0, tiled=True),
            lax.all_gather(proj_weight, "seq", axis=0, tiled=True),
            lax.all_gather(ln1_gain, "seq", axis=0, tiled=True),
            lax.all_gather(ln1_bias, "seq", axis=0, tiled=True),
            lax.all_gather(qv_bias, "seq", axis=1, tiled=True),
            lax.all_gather(out_bias, "seq", axis=0, tiled=True),
            lax.all_gather(ln2_gain, "seq", axis=0, tiled=True),
            lax.all_gather(ln2_bias, "seq", axis=0, tiled=True),
            lax.all_gather(fc_bias, "seq", axis=0, tiled=True),
            lax.all_gather(proj_bias, "seq", axis=0, tiled=True),
        )
        gain_one = gathered[4].astype(jnp.float32)
        shift_one = gathered[5].astype(jnp.float32)
        qv_full = gathered[6].astype(jnp.float32)
        out_shift = gathered[7].astype(jnp.float32)
        gain_two = gathered[8].astype(jnp.float32)
        shift_two = gathered[9].astype(jnp.float32)
        fc_shift = gathered[10].astype(jnp.float32)
        proj_shift = gathered[11].astype(jnp.float32)
        tokens_in = batch_tokens.reshape(row_count, width).astype(jnp.float32)
        normed_one = layer_norm(tokens_in, gain_one, shift_one).astype(jnp.bfloat16)
        packed_shift = jnp.concatenate([qv_full[0], jnp.zeros((width,), jnp.float32), qv_full[1]])
        packed = (spread_product(normed_one, gathered[0]) + packed_shift).astype(jnp.bfloat16)
        queries = packed[:, :width].reshape(group, local_len, heads, HEAD)
        key_local = packed[:, width : 2 * width].reshape(group, local_len, width)
        value_local = packed[:, 2 * width :].reshape(group, local_len, width)
        key_rows, value_rows = (
            lax.all_gather(key_local, "seq", axis=1, tiled=True),
            lax.all_gather(value_local, "seq", axis=1, tiled=True),
        )
        attended, log_total = lax.map(
            attend, (queries, key_rows, value_rows, batch_own, batch_places)
        )
        attended_low = attended.reshape(row_count, width).astype(jnp.bfloat16)
        middle = tokens_in + (spread_product(attended_low, gathered[1]) + out_shift)
        normed_two = layer_norm(middle, gain_two, shift_two).astype(jnp.bfloat16)
        hidden_pre = spread_product(normed_two, gathered[2]) + fc_shift
        hidden_low = smooth_gate(hidden_pre).astype(jnp.bfloat16)
        result = middle + (spread_product(hidden_low, gathered[3]) + proj_shift)
        outputs.append(result.astype(jnp.bfloat16).reshape(group, local_len, width))
        columns = (
            lax.all_gather(qkv_weight, "seq", axis=0, tiled=True),
            lax.all_gather(out_weight, "seq", axis=0, tiled=True),
            lax.all_gather(fc_weight, "seq", axis=0, tiled=True),
            lax.all_gather(proj_weight, "seq", axis=0, tiled=True),
        )
        grad_rows = batch_grad.reshape(row_count, width)
        grad_hidden = back_product(grad_rows, columns[3])
        grad_pre = gate_grad(hidden_pre, grad_hidden).astype(jnp.bfloat16)
        grad_normed_two = back_product(grad_pre, columns[2])
        grad_mid_norm, grad_gain_two, grad_shift_two = norm_grad(
            middle, gain_two, shift_two, grad_normed_two
        )
        grad_middle = grad_rows.astype(jnp.float32) + grad_mid_norm
        grad_branch = grad_middle.astype(jnp.bfloat16)
        grad_attended = back_product(grad_branch, columns[1]).astype(jnp.bfloat16)
        grad_attended = grad_attended.reshape(group, local_len, heads, HEAD)
        key_back, value_back = (
            lax.all_gather(key_local, "seq", axis=1, tiled=True),
            lax.all_gather(value_local, "seq", axis=1, tiled=True),
        )
        grad_queries, grad_keys, grad_values = lax.map(
            attend_back,
            (queries, key_back, value_back, batch_own, batch_places, log_total, grad_attended),
        )
        grad_keys, grad_values = (
            lax.psum_scatter(
                grad_keys.astype(jnp.bfloat16), "seq", scatter_dimension=1, tiled=True
            ).astype(jnp.float32),
            lax.psum_scatter(
                grad_values.astype(jnp.bfloat16), "seq", scatter_dimension=1, tiled=True
            ).astype(jnp.float32),
        )
        grad_packed = jnp.concatenate([grad_queries, grad_keys, grad_values], axis=-1)
        grad_packed = grad_packed.reshape(row_count, 3 * width).astype(jnp.bfloat16)
        grad_normed_one = back_product(grad_packed, columns[0])
        grad_in_norm, grad_gain_one, grad_shift_one = norm_grad(
            tokens_in, gain_one, shift_one, grad_normed_one
        )
        input_grads.append(
            (grad_middle + grad_in_norm).astype(jnp.bfloat16).reshape(group, local_len, width)
        )
        pairs = (
            (normed_one, grad_packed),
            (attended_low, grad_branch),
            (normed_two, grad_pre),
            (hidden_low, grad_rows),
        )
        for slot in range(4):
            left, right = pairs[slot]
            weight_sums[slot] = weight_sums[slot] + lax.dot_general(
                left, right, (((0,), (0,)), ((), ())), preferred_element_type=jnp.float32
            )
        qv_grad = jnp.stack(
            [
                jnp.sum(grad_packed[:, :width], axis=0, dtype=jnp.float32),
                jnp.sum(grad_packed[:, 2 * width :], axis=0, dtype=jnp.float32),
            ]
        )
        vector_terms = (
            grad_gain_one,
            grad_shift_one,
            qv_grad,
            jnp.sum(grad_branch, axis=0, dtype=jnp.float32),
            grad_gain_two,
            grad_shift_two,
            jnp.sum(grad_pre, axis=0, dtype=jnp.float32),
            jnp.sum(grad_rows, axis=0, dtype=jnp.float32),
        )
        vector_sums = [vector_sums[slot] + vector_terms[slot] for slot in range(8)]
    weight_parts = (
        lax.psum_scatter(
            weight_sums[0].astype(jnp.bfloat16), "dp", scatter_dimension=1, tiled=True
        ).astype(jnp.float32),
        lax.psum_scatter(
            weight_sums[1].astype(jnp.bfloat16), "dp", scatter_dimension=1, tiled=True
        ).astype(jnp.float32),
        lax.psum_scatter(
            weight_sums[2].astype(jnp.bfloat16), "dp", scatter_dimension=1, tiled=True
        ).astype(jnp.float32),
        lax.psum_scatter(
            weight_sums[3].astype(jnp.bfloat16), "dp", scatter_dimension=1, tiled=True
        ).astype(jnp.float32),
    )
    vector_parts = (
        lax.psum(vector_sums[0].astype(jnp.bfloat16), "dp").astype(jnp.float32),
        lax.psum(vector_sums[1].astype(jnp.bfloat16), "dp").astype(jnp.float32),
        lax.psum(vector_sums[2].astype(jnp.bfloat16), "dp").astype(jnp.float32),
        lax.psum(vector_sums[3].astype(jnp.bfloat16), "dp").astype(jnp.float32),
        lax.psum(vector_sums[4].astype(jnp.bfloat16), "dp").astype(jnp.float32),
        lax.psum(vector_sums[5].astype(jnp.bfloat16), "dp").astype(jnp.float32),
        lax.psum(vector_sums[6].astype(jnp.bfloat16), "dp").astype(jnp.float32),
        lax.psum(vector_sums[7].astype(jnp.bfloat16), "dp").astype(jnp.float32),
    )
    finals = (
        lax.psum_scatter(
            weight_parts[0].astype(jnp.bfloat16), "seq", scatter_dimension=0, tiled=True
        ).astype(jnp.float32),
        lax.psum_scatter(
            weight_parts[1].astype(jnp.bfloat16), "seq", scatter_dimension=0, tiled=True
        ).astype(jnp.float32),
        lax.psum_scatter(
            weight_parts[2].astype(jnp.bfloat16), "seq", scatter_dimension=0, tiled=True
        ).astype(jnp.float32),
        lax.psum_scatter(
            weight_parts[3].astype(jnp.bfloat16), "seq", scatter_dimension=0, tiled=True
        ).astype(jnp.float32),
        lax.psum_scatter(
            vector_parts[0].astype(jnp.bfloat16), "seq", scatter_dimension=0, tiled=True
        ).astype(jnp.float32),
        lax.psum_scatter(
            vector_parts[1].astype(jnp.bfloat16), "seq", scatter_dimension=0, tiled=True
        ).astype(jnp.float32),
        lax.psum_scatter(
            vector_parts[2].astype(jnp.bfloat16), "seq", scatter_dimension=1, tiled=True
        ).astype(jnp.float32),
        lax.psum_scatter(
            vector_parts[3].astype(jnp.bfloat16), "seq", scatter_dimension=0, tiled=True
        ).astype(jnp.float32),
        lax.psum_scatter(
            vector_parts[4].astype(jnp.bfloat16), "seq", scatter_dimension=0, tiled=True
        ).astype(jnp.float32),
        lax.psum_scatter(
            vector_parts[5].astype(jnp.bfloat16), "seq", scatter_dimension=0, tiled=True
        ).astype(jnp.float32),
        lax.psum_scatter(
            vector_parts[6].astype(jnp.bfloat16), "seq", scatter_dimension=0, tiled=True
        ).astype(jnp.float32),
        lax.psum_scatter(
            vector_parts[7].astype(jnp.bfloat16), "seq", scatter_dimension=0, tiled=True
        ).astype(jnp.float32),
    )
    return (
        jnp.concatenate(outputs, axis=0),
        jnp.concatenate(input_grads, axis=0),
        finals[0],
        finals[1],
        finals[2],
        finals[3],
        finals[4],
        finals[5],
        finals[6],
        finals[7],
        finals[8],
        finals[9],
        finals[10],
        finals[11],
    )


def solution(mesh):
    placed = (
        P("dp", "seq", None),
        P("dp", None),
        P("seq", "dp"),
        P("seq", "dp"),
        P("seq", "dp"),
        P("seq", "dp"),
        P("seq"),
        P("seq"),
        P(None, "seq"),
        P("seq"),
        P("seq"),
        P("seq"),
        P("seq"),
        P("seq"),
        P("dp", "seq", None),
    )
    return jax.shard_map(
        local,
        mesh=mesh,
        in_specs=placed,
        out_specs=(
            P("dp", "seq", None),
            P("dp", "seq", None),
            P("seq", "dp"),
            P("seq", "dp"),
            P("seq", "dp"),
            P("seq", "dp"),
            P("seq"),
            P("seq"),
            P(None, "seq"),
            P("seq"),
            P("seq"),
            P("seq"),
            P("seq"),
            P("seq"),
        ),
        check_vma=False,
    )
```

profile of v0, /device:TPU:0, one launch (start us, length us, event | category | flops | bytes accessed | tf_op | source)
XLA Modules:
  0.0 2959.0 jit_solution(15673766511900247258)
XLA Ops:
  8.1 26.6 all-gather.18.cloned.1.call-done
  62.0 194.7 %all-gather.20.cloned.1.call-done = bf16[1600,4800]{0,1:T(8,128)(2,1)} async-done(((bf16[1600,600]{0,1:T(8,128)(2,1)}), bf16[1600,4800]{0,1:T(8,128)(2,1)}) %all-gather.20.cloned.1.call-update) | async-done | bytes 15360016 | tf_op jit(solution)/shard_map/all_gather | solution.py:41
  327.2 19.5 all-gather.32.cloned.1.call-done
  393.0 75.0 %all-gather.22.cloned.1.call-done = bf16[1600,1600]{0,1:T(8,128)(2,1)} async-done(((bf16[1600,200]{0,1:T(8,128)(2,1)}), bf16[1600,1600]{0,1:T(8,128)(2,1)}) %all-gather.22.cloned.1.call-update) | async-done | bytes 5120016 | tf_op jit(solution)/shard_map/all_gather | solution.py:41
  473.9 24.1 all-gather.36.cloned.1.call-done
  550.7 388.5 %all-gather.26.cloned.1.call-done = bf16[1600,6400]{0,1:T(8,128)(2,1)} async-done(((bf16[1600,800]{0,1:T(8,128)(2,1)}), bf16[1600,6400]{0,1:T(8,128)(2,1)}) %all-gather.26.cloned.1.call-update) | async-done | bytes 20480016 | tf_op jit(solution)/shard_map/all_gather | solution.py:41
  952.8 380.6 %all-gather.28.cloned.1.call-done = bf16[6400,1600]{0,1:T(8,128)(2,1)} async-done(((bf16[6400,200]{0,1:T(8,128)(2,1)}), bf16[6400,1600]{0,1:T(8,128)(2,1)}) %all-gather.28.cloned.1.call-update) | async-done | bytes 20480016 | tf_op jit(solution)/shard_map/all_gather | solution.py:41
  1378.7 18.0 convert_reduce_fusion
  1396.7 17.7 multiply_reduce_fusion.2
  1437.7 21.6 multiply_reduce_fusion.1
  1459.3 18.2 multiply_convert_fusion.1
  1503.9 20.8 multiply_reduce_fusion
  1524.8 20.1 multiply_convert_fusion
  1604.4 20.0 add_convert_fusion.2
  1625.8 19.0 fusion.100
  1644.8 23.5 add_convert_fusion.1
  1669.8 19.3 fusion.156
  1689.1 23.4 add_convert_fusion
  1733.7 308.8 %reduce-scatter.51.cloned.1.call-done = bf16[1600,600]{0,1:T(8,128)(2,1)} async-done(((bf16[1600,4800]{0,1:T(8,128)(2,1)}), bf16[1600,600]{0,1:T(8,128)(2,1)}) %reduce-scatter.51.cloned.1.call-update) | async-done | bytes 1920016
  2048.5 385.4 %reduce-scatter.55.cloned.1.call-done = bf16[6400,200]{0,1:T(8,128)(2,1)} async-done(((bf16[6400,1600]{0,1:T(8,128)(2,1)}), bf16[6400,200]{0,1:T(8,128)(2,1)}) %reduce-scatter.55.cloned.1.call-update) | async-done | bytes 2560016
  2488.1 297.1 %reduce-scatter.39.cloned.1.call-done = bf16[1600,800]{0,1:T(8,128)(2,1)} async-done(((bf16[1600,6400]{0,1:T(8,128)(2,1)}), bf16[1600,800]{0,1:T(8,128)(2,1)}) %reduce-scatter.39.cloned.1.call-update) | async-done | bytes 2560016 | tf_op jit(solution)/shard_map/reduce_scatter | solution.py:283
  2822.3 35.2 %all-reduce.17 = (bf16[400]{0:T(512)(128)(2,1)S(1)}, bf16[400]{0:T(512)(128)(2,1)S(1)}, bf16[2,400]{1,0:T(2,128)(2,1)S(1)}, bf16[400]{0:T(512)(128)(2,1)S(1)}, b...) all-reduce(bf16[400]{0:T(512)(128)(2,1)S(1)} %dynamic-slice.14, ...), channel_id=1, replica_groups=mesh['dp'=8,'seq'=4] {'dp'}, use_global_device_ids=true, to_apply=%region_37.38 | all-reduce | flops 4800 | bytes 19200 | tf_op jit(solution)/shard_map/psum | solution.py:291
  2871.2 38.9 %reduce-scatter.47.cloned.1.call-done = bf16[1600,200]{1,0:T(8,128)(2,1)} async-done(((bf16[6400,200]{1,0:T(8,128)(2,1)}), bf16[1600,200]{1,0:T(8,128)(2,1)}) %reduce-scatter.47.cloned.1.call-update) | async-done | bytes 640016
  2912.8 36.2 %reduce-scatter.45.cloned.1.call-done = bf16[400,800]{1,0:T(8,128)(2,1)} async-done(((bf16[1600,800]{1,0:T(8,128)(2,1)}), bf16[400,800]{1,0:T(8,128)(2,1)}) %reduce-scatter.45.cloned.1.call-update) | async-done | bytes 640016
  (398 shorter events, 507.7 us)
Async XLA Ops:
  7.2 27.4 all-gather.18.cloned.1.call-start
  8.0 248.7 %all-gather.20.cloned.1.call-start = ((), (), s32[]{:S(2)}) async-start(), calls=%async_computation.14 | async-start | bytes 17971200 | tf_op jit(solution)/shard_map/all_gather | solution.py:41
  38.7 258.2 %all-gather.24.cloned.1.call-start = ((), (), s32[]{:S(2)}) async-start(), calls=%async_computation.16 | async-start | bytes 3584000 | tf_op jit(solution)/shard_map/all_gather | solution.py:166
  39.5 275.6 %all-gather.38.cloned.1.call-start = ((), (), s32[]{:S(2)}) async-start(), calls=%async_computation.28 | async-start | bytes 3328000 | tf_op jit(solution)/shard_map/all_gather | solution.py:167
  40.0 306.7 %all-gather.32.cloned.1.call-start = ((), (), s32[]{:S(2)}) async-start(), calls=%async_computation.25 | async-start | bytes 4096000 | tf_op jit(solution)/shard_map/all_gather | solution.py:193
  268.4 110.0 %all-gather.30.cloned.1.call-start = ((), (), s32[]{:S(2)}) async-start(), calls=%async_computation.24 | async-start | bytes 4096000 | tf_op jit(solution)/shard_map/all_gather | solution.py:194
  269.0 199.0 %all-gather.22.cloned.1.call-start = ((), (), s32[]{:S(2)}) async-start(), calls=%async_computation.15 | async-start | bytes 5990400 | tf_op jit(solution)/shard_map/all_gather | solution.py:41
  283.8 214.2 %all-gather.36.cloned.1.call-start = ((), (), s32[]{:S(2)}) async-start(), calls=%async_computation.27 | async-start | bytes 4096000 | tf_op jit(solution)/shard_map/all_gather | solution.py:193
  296.1 233.8 %all-gather.34.cloned.1.call-start = ((), (), s32[]{:S(2)}) async-start(), calls=%async_computation.26 | async-start | bytes 4096000 | tf_op jit(solution)/shard_map/all_gather | solution.py:194
  296.8 642.4 %all-gather.26.cloned.1.call-start = ((), (), s32[]{:S(2)}) async-start(), calls=%async_computation.17 | async-start | bytes 23961600 | tf_op jit(solution)/shard_map/all_gather | solution.py:41
  302.3 1031.1 %all-gather.28.cloned.1.call-start = ((), (), s32[]{:S(2)}) async-start(), calls=%async_computation.18 | async-start | bytes 23040000 | tf_op jit(solution)/shard_map/all_gather | solution.py:41
  324.9 1255.1 %reduce-scatter.33.cloned.1.call-start = ((), (), s32[]{:S(2)}) async-start(), calls=%async_computation.20 | async-start | bytes 4096000 | tf_op jit(solution)/shard_map/reduce_scatter | solution.py:235
  1437.7 142.4 %reduce-scatter.31.cloned.1.call-start = ((), (), s32[]{:S(2)}) async-start(), calls=%async_computation.19 | async-start | bytes 4096000 | tf_op jit(solution)/shard_map/reduce_scatter | solution.py:232
  1483.2 113.9 %reduce-scatter.37.cloned.1.call-start = ((), (), s32[]{:S(2)}) async-start(), calls=%async_computation.22 | async-start | bytes 4096000 | tf_op jit(solution)/shard_map/reduce_scatter | solution.py:235
  1503.9 100.5 %reduce-scatter.35.cloned.1.call-start = ((), (), s32[]{:S(2)}) async-start(), calls=%async_computation.21 | async-start | bytes 4096000 | tf_op jit(solution)/shard_map/reduce_scatter | solution.py:232
  1550.6 180.7 %reduce-scatter.53.cloned.1.call-start = ((), (), s32[]{:S(2)}) async-start(), calls=%async_computation.35 | async-start | bytes 5990400
  1557.6 485.0 %reduce-scatter.51.cloned.1.call-start = ((), (), s32[]{:S(2)}) async-start(), calls=%async_computation.34 | async-start | bytes 17971200
  1624.4 809.4 %reduce-scatter.55.cloned.1.call-start = ((), (), s32[]{:S(2)}) async-start(), calls=%async_computation.36 | async-start | bytes 23040000
  1668.4 1116.8 %reduce-scatter.39.cloned.1.call-start = ((), (), s32[]{:S(2)}) async-start(), calls=%async_computation.23 | async-start | bytes 23961600 | tf_op jit(solution)/shard_map/reduce_scatter | solution.py:283
  1712.5 1108.8 %reduce-scatter.49.cloned.1.call-start = ((), (), s32[]{:S(2)}) async-start(), calls=%async_computation.33 | async-start | bytes 512000
  1716.8 1145.3 %reduce-scatter.43.cloned.1.call-start = ((), (), s32[]{:S(2)}) async-start(), calls=%async_computation.30 | async-start | bytes 1024000
  1733.7 1135.1 %reduce-scatter.41.cloned.1.call-start = ((), (), s32[]{:S(2)}) async-start(), calls=%async_computation.29 | async-start | bytes 2560000
  2046.6 863.5 %reduce-scatter.47.cloned.1.call-start = ((), (), s32[]{:S(2)}) async-start(), calls=%async_computation.32 | async-start | bytes 4096000
  2438.5 510.4 %reduce-scatter.45.cloned.1.call-start = ((), (), s32[]{:S(2)}) async-start(), calls=%async_computation.31 | async-start | bytes 3584000
  (95 other events, 13613.0 us)
Sparse Core Ops, SparseCore 0:
  9.6 25.0 all-gather.17
  38.8 217.7 all-gather.19
  258.2 29.5 all-gather.23
  289.2 25.7 all-gather.37
  317.0 29.6 all-gather.31
  348.7 29.6 all-gather.29
  380.7 87.2 all-gather.21
  470.1 27.8 all-gather.35
  500.2 29.6 all-gather.33
  531.3 407.9 all-gather.25
  940.8 392.5 all-gather.27
  1437.8 38.7 reduce-scatter.32
  1483.3 38.4 reduce-scatter.30
  1524.2 38.7 reduce-scatter.36
  1565.6 38.7 reduce-scatter.34
  1607.7 123.5 reduce-scatter.52
  1733.6 308.8 reduce-scatter.50
  2046.0 387.8 reduce-scatter.54
  2437.5 347.6 reduce-scatter.38
  2788.2 20.0 reduce-scatter.48
  2811.3 23.4 reduce-scatter.42
  2837.6 31.1 reduce-scatter.40
  2871.3 38.7 reduce-scatter.46
  2912.7 36.1 reduce-scatter.44
where the time goes:
time: 2970 us; the launch traced here: 2960 us
  waiting for transfers between devices  2220 us (75%)
  matrix products  479 us (16%)
  other arithmetic  93.2 us (3%)
  blocking collectives  77.4 us (3%)
  local copies, waits for them, and re-layouts  64.3 us (2%)
    all_gather x4, waiting for transfers between devices, spread_product(): lax.all_gather(columns, 'dp', axis=1, tiled=True)  1040 us
    unnamed x32, waiting for transfers between devices  792 us
    reduce_scatter x1, waiting for transfers between devices, local(): lax.psum_scatter(weight_sums[2].astype(jnp.bfloat16), 'dp', scatter_dimen...  297 us
    dot_general x8, matrix products, local(): lax.dot_general(left, right, (((0,), (0,)), ((), ())), preferred_element_...  128 us
    dot_general x8, matrix products, back_product(): lax.dot_general(grads, lax.all_gather(columns, 'dp', axis=1, tiled=True),...  105 us
    dot_general x8, matrix products, spread_product(): jnp.dot(left, lax.all_gather(columns, 'dp', axis=1, tiled=True), preferre...  86 us
  transfers between devices with their start and end apart: 24, of which 18 were waited for; matrix products, arithmetic and copies ran while one was open for 17% of the time, Pallas kernels for 0%

commit v1 on v0

--- a/solution.py
+++ b/solution.py
@@ -1,6 +1,10 @@
+import functools
+
 import jax
 import jax.numpy as jnp
 from jax import lax
+from jax.experimental import pallas as pl
+from jax.experimental.pallas import tpu as pltpu
 from jax.sharding import PartitionSpec as P
 
 HEAD = 64
@@ -353,6 +357,520 @@
     )
 
 
+BF = jnp.bfloat16
+F32 = jnp.float32
+PAIR = 2 * HEAD
+NEG = -1e30
+
+
+def mm(left, right, contract):
+    return lax.dot_general(left, right, (contract, ((), ())), preferred_element_type=F32)
+
+
+def nn(left, right):
+    return mm(left, right, ((1,), (0,)))
+
+
+def nt(left, right):
+    return mm(left, right, ((1,), (1,)))
+
+
+def tn(left, right):
+    return mm(left, right, ((0,), (0,)))
+
+
+def sort_rows(pos_ref, src, dst, chunk, count):
+    for j in range(count):
+        dst[pl.ds(j * chunk, chunk), :] = src[
+            pl.ds(pl.multiple_of(pos_ref[j] * chunk, chunk), chunk), :
+        ]
+
+
+def take_rows(pos_ref, src, first, chunk, count):
+    parts = [
+        src[pl.ds(pl.multiple_of(pos_ref[first + j] * chunk, chunk), chunk), :]
+        for j in range(count)
+    ]
+    return jnp.concatenate(parts, axis=0)
+
+
+def put_rows(pos_ref, dst, first, chunk, count, value):
+    for j in range(count):
+        dst[pl.ds(pl.multiple_of(pos_ref[first + j] * chunk, chunk), chunk), :] = value[
+            j * chunk : (j + 1) * chunk
+        ]
+
+
+def head_lanes(value, head):
+    lane = lax.broadcasted_iota(jnp.int32, value.shape, 1)
+    inside = (lane < HEAD) if head == 0 else (lane >= HEAD)
+    return jnp.where(inside, value, jnp.zeros_like(value))
+
+
+def causal(block):
+    key = lax.broadcasted_iota(jnp.int32, block.shape, 0)
+    query = lax.broadcasted_iota(jnp.int32, block.shape, 1)
+    return key <= query
+
+
+def attend_kernel(
+    chunk, count, step, pos_ref, keep_ref, q_ref, k_ref, v_ref, o_ref, lse_ref, ks, vt
+):
+    pair = pl.program_id(0)
+    sort_rows(pos_ref, k_ref, ks, chunk, count)
+    for j in range(count):
+        rows = v_ref[pl.ds(pl.multiple_of(pos_ref[j] * chunk, chunk), chunk), :]
+        vt[:, pl.ds(j * chunk, chunk)] = rows.T
+    tile = step * chunk
+    for block in range(count // step):
+        q_rows = take_rows(pos_ref, q_ref, block * step, chunk, step) * HEAD ** (-0.5)
+        start = block * tile
+        done = []
+        for head in range(2):
+            q_head = head_lanes(q_rows.astype(BF), head)
+            diag = nt(ks[pl.ds(start, tile), :], q_head)
+            diag = jnp.where(causal(diag), diag, NEG)
+            top = jnp.max(diag, axis=0, keepdims=True)
+            if block > 0:
+                full = nt(ks[pl.ds(0, start), :], q_head)
+                top = jnp.maximum(top, jnp.max(full, axis=0, keepdims=True))
+            p_diag = jnp.exp(diag - top)
+            total = jnp.sum(p_diag, axis=0, keepdims=True)
+            out = nn(vt[:, pl.ds(start, tile)], p_diag.astype(BF))
+            if block > 0:
+                p_full = jnp.exp(full - top)
+                total = total + jnp.sum(p_full, axis=0, keepdims=True)
+                out = out + nn(vt[:, pl.ds(0, start)], p_full.astype(BF))
+            lse_ref[pl.ds(head, 1), pl.ds(start, tile)] = top + jnp.log(total)
+            out = out / total
+            done.append(jnp.where(keep_ref[2 * pair + head] > 0, out, jnp.zeros_like(out)))
+        merged = jnp.concatenate([done[0][:HEAD], done[1][HEAD:]], axis=0)
+        put_rows(pos_ref, o_ref, block * step, chunk, step, merged.T.astype(BF))
+
+
+def attend_back_kernel(
+    chunk,
+    count,
+    step,
+    pos_ref,
+    keep_ref,
+    q_ref,
+    k_ref,
+    v_ref,
+    do_ref,
+    lse_ref,
+    dq_ref,
+    dk_ref,
+    dv_ref,
+    ks,
+    vs,
+    kt,
+    dks,
+    dvs,
+):
+    pair = pl.program_id(0)
+    sort_rows(pos_ref, k_ref, ks, chunk, count)
+    sort_rows(pos_ref, v_ref, vs, chunk, count)
+    for j in range(count):
+        kt[:, pl.ds(j * chunk, chunk)] = ks[pl.ds(j * chunk, chunk), :].T
+    tile = step * chunk
+    for block in range(count // step):
+        q_rows = (take_rows(pos_ref, q_ref, block * step, chunk, step) * HEAD ** (-0.5)).astype(BF)
+        do_rows = take_rows(pos_ref, do_ref, block * step, chunk, step)
+        start = block * tile
+        dq = []
+        for head in range(2):
+            q_head = head_lanes(q_rows, head)
+            do_head = head_lanes(do_rows, head)
+            do_head = jnp.where(keep_ref[2 * pair + head] > 0, do_head, jnp.zeros_like(do_head))
+            lse = lse_ref[pl.ds(head, 1), pl.ds(start, tile)]
+            spans = [(start, tile)] if block == 0 else [(0, start), (start, tile)]
+            probs = []
+            grads = []
+            delta = jnp.zeros_like(lse)
+            for first, size in spans:
+                s = nt(ks[pl.ds(first, size), :], q_head)
+                p = jnp.exp(s - lse)
+                if first == start:
+                    p = jnp.where(causal(p), p, jnp.zeros_like(p))
+                g = nt(vs[pl.ds(first, size), :], do_head)
+                delta = delta + jnp.sum(p * g, axis=0, keepdims=True)
+                probs.append(p)
+                grads.append(g)
+            dq_head = jnp.zeros((PAIR, tile), F32)
+            for (first, size), p, g in zip(spans, probs, grads):
+                ds = (p * (g - delta)).astype(BF)
+                dq_head = dq_head + nn(kt[:, pl.ds(first, size)], ds)
+                dk = nn(ds, q_head)
+                dv = nn(p.astype(BF), do_head)
+                if first == start and head == 0:
+                    dks[pl.ds(first, size), :] = dk
+                    dvs[pl.ds(first, size), :] = dv
+                else:
+                    dks[pl.ds(first, size), :] += dk
+                    dvs[pl.ds(first, size), :] += dv
+            dq.append(dq_head)
+        merged = jnp.concatenate([dq[0][:HEAD], dq[1][HEAD:]], axis=0) * HEAD ** (-0.5)
+        put_rows(pos_ref, dq_ref, block * step, chunk, step, merged.T.astype(BF))
+    put_rows(pos_ref, dk_ref, 0, chunk, count, dks[...].astype(BF))
+    put_rows(pos_ref, dv_ref, 0, chunk, count, dvs[...].astype(BF))
+
+
+def attend_fast(pos, keep, queries, keys, values):
+    length, wide = queries.shape
+    count = pos.shape[0]
+    chunk = length // count
+    pairs = wide // PAIR
+    tile = pl.BlockSpec((length, PAIR), lambda p, *_: (0, p))
+    return pl.pallas_call(
+        functools.partial(attend_kernel, chunk, count, 2),
+        out_shape=(
+            jax.ShapeDtypeStruct((length, wide), BF),
+            jax.ShapeDtypeStruct((pairs * 8, length), F32),
+        ),
+        grid_spec=pltpu.PrefetchScalarGridSpec(
+            num_scalar_prefetch=2,
+            grid=(pairs,),
+            in_specs=[tile, tile, tile],
+            out_specs=[tile, pl.BlockSpec((8, length), lambda p, *_: (p, 0))],
+            scratch_shapes=[pltpu.VMEM((length, PAIR), BF), pltpu.VMEM((PAIR, length), BF)],
+        ),
+        cost_estimate=pl.CostEstimate(
+            flops=4 * length * length * wide,
+            transcendentals=length * length * wide // PAIR,
+            bytes_accessed=8 * length * wide,
+        ),
+        name="attend",
+    )(pos, keep, queries, keys, values)
+
+
+def attend_back_fast(pos, keep, queries, keys, values, grad_out, lse):
+    length, wide = queries.shape
+    count = pos.shape[0]
+    chunk = length // count
+    pairs = wide // PAIR
+    tile = pl.BlockSpec((length, PAIR), lambda p, *_: (0, p))
+    return pl.pallas_call(
+        functools.partial(attend_back_kernel, chunk, count, 2),
+        out_shape=(jax.ShapeDtypeStruct((length, wide), BF),) * 3,
+        grid_spec=pltpu.PrefetchScalarGridSpec(
+            num_scalar_prefetch=2,
+            grid=(pairs,),
+            in_specs=[tile, tile, tile, tile, pl.BlockSpec((8, length), lambda p, *_: (p, 0))],
+            out_specs=[tile, tile, tile],
+            scratch_shapes=[
+                pltpu.VMEM((length, PAIR), BF),
+                pltpu.VMEM((length, PAIR), BF),
+                pltpu.VMEM((PAIR, length), BF),
+                pltpu.VMEM((length, PAIR), F32),
+                pltpu.VMEM((length, PAIR), F32),
+            ],
+        ),
+        cost_estimate=pl.CostEstimate(
+            flops=10 * length * length * wide,
+            transcendentals=length * length * wide // PAIR,
+            bytes_accessed=16 * length * wide,
+        ),
+        name="attend_back",
+    )(pos, keep, queries, keys, values, grad_out, lse)
+
+
+def piece_sizes(total, parts):
+    granules = total // 8
+    return [8 * (granules // parts + (1 if i < granules % parts else 0)) for i in range(parts)]
+
+
+def to_slots(rows, parts):
+    sizes = piece_sizes(rows.shape[0], parts)
+    slot = max(sizes)
+    out = []
+    first = 0
+    for size in sizes:
+        piece = rows[first : first + size]
+        if size < slot:
+            piece = jnp.concatenate([piece, jnp.zeros((slot - size,) + rows.shape[1:], rows.dtype)])
+        out.append(piece)
+        first += size
+    return jnp.stack(out)
+
+
+def from_slots(slots, total):
+    sizes = piece_sizes(total, slots.shape[-3])
+    return jnp.concatenate(
+        [slots[..., i, :size, :] for i, size in enumerate(sizes)], axis=-2
+    )
+
+
+def swap_core(value):
+    count = lax.axis_size("seq")
+    return lax.ppermute(value, "seq", [(i, i ^ 1) for i in range(count)])
+
+
+def swap_y(value):
+    count = lax.axis_size("seq")
+    return lax.ppermute(value, "seq", [(i, i ^ 2) for i in range(count)])
+
+
+def gather_four(value):
+    near = swap_core(value)
+    far = swap_y(value)
+    return jnp.concatenate([value, near, far, swap_core(far)], axis=0)
+
+
+def reduce_two(part):
+    half = part.shape[0] // 2
+    return part[:half] + swap_core(part[half:].astype(BF)).astype(F32)
+
+
+def reduce_four(part):
+    n = part.shape[0] // 4
+    send = jnp.concatenate([part[n : 2 * n], part[3 * n :]], axis=0).astype(BF)
+    kept = jnp.concatenate([part[:n], part[2 * n : 3 * n]], axis=0)
+    both = kept + swap_core(send).astype(F32)
+    return both[:n] + swap_y(both[n:].astype(BF)).astype(F32)
+
+
+def local_fast(
+    tokens,
+    span_order,
+    qkv_weight,
+    out_weight,
+    fc_weight,
+    proj_weight,
+    ln1_gain,
+    ln1_bias,
+    qv_bias,
+    out_bias,
+    ln2_gain,
+    ln2_bias,
+    fc_bias,
+    proj_bias,
+    out_grad,
+):
+    seqs = lax.axis_size("seq")
+    dps = lax.axis_size("dp")
+    rank = lax.axis_index("seq")
+    y = rank // 2
+    core = rank % 2
+    local_len = tokens.shape[1]
+    width = tokens.shape[2]
+    full_len = local_len * seqs
+    count = span_order.shape[1]
+    heads = width // HEAD
+    core_heads = (heads + 1) // 2
+    slots = core_heads + core_heads % 2
+    wide = slots * HEAD
+    skip = (heads - core_heads) * HEAD
+    hid = fc_weight.shape[1] // seqs
+    pcols = proj_weight.shape[1]
+    blocks = proj_weight.shape[0] // (seqs * hid)
+
+    def pick(zero, one):
+        return jnp.where(core == 0, zero, one)
+
+    qkv_slots = to_slots(qkv_weight.T, seqs)
+    out_slots = to_slots(out_weight.T, seqs)
+    qs = qkv_slots.shape[1]
+    os = out_slots.shape[1]
+    first = lax.all_to_all(
+        jnp.concatenate([qkv_slots, out_slots], axis=1), "seq", 0, 0
+    )
+    first = first.transpose(1, 0, 2).reshape(qs + os, width)
+    first_all = lax.all_gather(first, ("dp", "seq"), axis=0).reshape(dps, seqs, qs + os, width)
+    qkv_t = from_slots(first_all[:, :, :qs], qkv_weight.shape[1]).reshape(3, width, width)
+    out_t = from_slots(first_all[:, :, qs:], out_weight.shape[1]).reshape(width, width)
+
+    fc_pieces = fc_weight.T.reshape(seqs, hid, fc_weight.shape[0])
+    proj_pieces = (
+        proj_weight.T.reshape(pcols, blocks, seqs, hid)
+        .transpose(2, 0, 1, 3)
+        .reshape(seqs, pcols, blocks * hid)
+    )
+    second = lax.all_to_all(jnp.concatenate([fc_pieces, proj_pieces], axis=1), "seq", 0, 0)
+    second = second.transpose(1, 0, 2).reshape(hid + pcols, width)
+    fc_t = lax.all_gather(second[:hid], "dp", axis=0, tiled=True)
+    proj_t = lax.all_gather(second[hid:], "dp", axis=0, tiled=True)
+
+    vectors = jnp.concatenate(
+        [ln1_gain, ln1_bias, qv_bias[0], qv_bias[1], out_bias, ln2_gain, ln2_bias, proj_bias, fc_bias]
+    )
+    vectors = lax.all_gather(vectors, "seq", axis=0)
+    piece = ln1_gain.shape[0]
+    gain_one, shift_one, q_shift, v_shift, out_shift, gain_two, shift_two, proj_shift = [
+        vectors[:, i * piece : (i + 1) * piece].reshape(-1).astype(F32) for i in range(8)
+    ]
+    fc_all = vectors[:, 8 * piece :].reshape(dps, seqs, hid)
+    fc_shift = lax.dynamic_index_in_dim(fc_all, rank, 1, False).reshape(-1).astype(F32)
+
+    def own_rows(value):
+        mine = lax.dynamic_index_in_dim(value, y, 0, False)
+        other = lax.dynamic_index_in_dim(value, 1 - y, 0, False)
+        return jnp.concatenate([mine, swap_y(other)], axis=0)
+
+    def native_rows(value):
+        mine, other = value[:local_len], swap_y(value[local_len:])
+        return jnp.where(y == 0, jnp.stack([mine, other]), jnp.stack([other, mine]))
+
+    tok = own_rows(tokens).astype(F32)
+    grad_rows = own_rows(out_grad)
+    grad_all = gather_four(grad_rows)
+    ranks = jnp.stack([2 * y + core, 2 * (1 - y) + core, 2 * y + 1 - core, 2 * (1 - y) + 1 - core])
+    per = count // seqs
+    storage = (ranks[:, None] * per + jnp.arange(per, dtype=jnp.int32)[None]).reshape(-1)
+    own_order = lax.dynamic_index_in_dim(span_order, y, 0, False)
+    ids = jnp.arange(count, dtype=jnp.int32)
+    held = jnp.sum(jnp.where(storage[:, None] == ids[None], own_order[None], 0), axis=1)
+    pos = jnp.sum(jnp.where(held[None] == ids[:, None], ids[None], 0), axis=1).astype(jnp.int32)
+    slot_ids = jnp.arange(slots, dtype=jnp.int32)
+    keep = jnp.where(core == 0, slot_ids < core_heads, (slot_ids < core_heads) & (slot_ids >= 2 * core_heads - heads))
+    keep = keep.astype(jnp.int32)
+
+    normed_one = layer_norm(tok, gain_one, shift_one).astype(BF)
+    normed_one = jnp.concatenate([normed_one, swap_core(normed_one)], axis=0)
+    pad = jnp.zeros((skip + wide - width, width), BF)
+    w_heads = []
+    for i in range(3):
+        rows = jnp.concatenate([qkv_t[i], pad], axis=0)
+        w_heads.append(pick(rows[:wide], rows[skip : skip + wide]))
+    w_core = jnp.concatenate(w_heads, axis=0)
+
+    def core_vector(value):
+        value = jnp.concatenate([value, jnp.zeros((skip + wide - width,), F32)])
+        return pick(value[:wide], value[skip : skip + wide])
+
+    b_core = jnp.concatenate([core_vector(q_shift), jnp.zeros((wide,), F32), core_vector(v_shift)])
+    packed = (nt(normed_one, w_core) + b_core).astype(BF)
+    queries, keys, values = packed[:, :wide], packed[:, wide : 2 * wide], packed[:, 2 * wide :]
+    attended, lse = attend_fast(pos, keep, queries, keys, values)
+    out_pad = jnp.concatenate([out_t, pad.T], axis=1)
+    out_core = pick(out_pad[:, :wide], out_pad[:, skip : skip + wide])
+    middle = tok + (reduce_two(nt(attended, out_core)) + out_shift)
+    normed_two = layer_norm(middle, gain_two, shift_two).astype(BF)
+
+    normed_all = gather_four(normed_two)
+    hidden_pre = nt(normed_all, fc_t) + fc_shift
+    hidden = smooth_gate(hidden_pre).astype(BF)
+    grad_hidden = nt(grad_all, proj_t.T)
+    grad_pre = gate_grad(hidden_pre, grad_hidden).astype(BF)
+    grad_normed_two = reduce_four(nn(grad_pre, fc_t))
+    proj_grad = tn(grad_all, hidden)
+    fc_grad = tn(grad_pre, normed_all)
+    result = middle + (reduce_four(nt(hidden, proj_t)) + proj_shift)
+    output = native_rows(result.astype(BF))
+    proj_part = lax.psum_scatter(proj_grad.astype(BF), "dp", scatter_dimension=0, tiled=True)
+    fc_part = lax.psum_scatter(fc_grad.astype(BF), "dp", scatter_dimension=0, tiled=True)
+
+    grad_mid_norm, grad_gain_two, grad_shift_two = norm_grad(
+        middle, gain_two, shift_two, grad_normed_two
+    )
+    grad_middle = grad_rows.astype(F32) + grad_mid_norm
+    grad_branch = grad_middle.astype(BF)
+    branch_all = jnp.concatenate([grad_branch, swap_core(grad_branch)], axis=0)
+    grad_attended = nn(branch_all, out_core).astype(BF)
+    out_grad_core = tn(branch_all, attended)
+    grad_q, grad_k, grad_v = attend_back_fast(
+        pos, keep, queries, keys, values, grad_attended, lse
+    )
+    grad_packed = jnp.concatenate([grad_q, grad_k, grad_v], axis=1)
+    qkv_grad_core = tn(grad_packed, normed_one).astype(BF)
+    grad_normed_one = reduce_two(nn(grad_packed, w_core))
+    grad_in_norm, grad_gain_one, grad_shift_one = norm_grad(
+        tok, gain_one, shift_one, grad_normed_one
+    )
+    input_grad = native_rows((grad_middle + grad_in_norm).astype(BF))
+
+    valid = core_heads * HEAD
+    low = 2 * valid - width
+
+    def both_cores(mine, other, axis):
+        def cut(value, a, b):
+            return lax.slice_in_dim(value, a, b, axis=axis)
+
+        return pick(
+            jnp.concatenate([cut(mine, 0, valid), cut(other, low, valid)], axis=axis),
+            jnp.concatenate([cut(other, 0, valid), cut(mine, low, valid)], axis=axis),
+        )
+
+    other_qkv = swap_core(qkv_grad_core)
+    qkv_full = jnp.concatenate(
+        [
+            both_cores(
+                qkv_grad_core[i * wide : (i + 1) * wide], other_qkv[i * wide : (i + 1) * wide], 0
+            )
+            for i in range(3)
+        ],
+        axis=0,
+    )
+    out_low = out_grad_core.astype(BF)
+    out_full = both_cores(out_low, swap_core(out_low), 1)
+    send = jnp.concatenate(
+        [
+            jax.vmap(lambda rows: to_slots(rows, seqs))(qkv_full.reshape(dps, -1, width)),
+            jax.vmap(lambda rows: to_slots(rows, seqs))(out_full.reshape(dps, -1, width)),
+        ],
+        axis=2,
+    )
+    keep_core = jnp.arange(seqs, dtype=jnp.int32) % 2 == core
+    send = jnp.where(keep_core[None, :, None, None], send, jnp.zeros_like(send))
+    first_part = lax.psum_scatter(
+        send.reshape(dps * seqs * (qs + os), width), ("dp", "seq"), scatter_dimension=0, tiled=True
+    )
+
+    def spread(value):
+        rows = value.shape[0]
+        return lax.all_to_all(value.reshape(rows, seqs, -1).transpose(1, 0, 2), "seq", 0, 0)
+
+    first_back = spread(first_part)
+    qkv_weight_grad = from_slots(first_back[:, :qs], qkv_weight.shape[1]).T.astype(F32)
+    out_weight_grad = from_slots(first_back[:, qs:], out_weight.shape[1]).T.astype(F32)
+    fc_back = spread(fc_part)
+    fc_weight_grad = fc_back.reshape(seqs * hid, -1).T.astype(F32)
+    proj_back = spread(proj_part).reshape(seqs, pcols, blocks, hid)
+    proj_weight_grad = proj_back.transpose(2, 0, 3, 1).reshape(-1, pcols).astype(F32)
+
+    gq = jnp.sum(grad_q, axis=0, dtype=F32)[:valid]
+    gv = jnp.sum(grad_v, axis=0, dtype=F32)[:valid]
+
+    def whole(value):
+        return pick(
+            jnp.concatenate([value, jnp.zeros((width - valid,), F32)]),
+            jnp.concatenate([jnp.zeros((width - valid,), F32), value]),
+        )
+
+    gf = jnp.sum(grad_pre, axis=0, dtype=F32).reshape(dps, 1, hid)
+    gf = jnp.where(jnp.arange(seqs, dtype=jnp.int32)[None, :, None] == rank, gf, 0.0)
+    rows = [
+        grad_gain_one,
+        grad_shift_one,
+        whole(gq),
+        whole(gv),
+        jnp.sum(grad_branch, axis=0, dtype=F32),
+        grad_gain_two,
+        grad_shift_two,
+        jnp.sum(grad_rows, axis=0, dtype=F32),
+    ]
+    summed = lax.psum(jnp.concatenate(rows + [gf.reshape(-1)]), ("dp", "seq"))
+    mats = summed[: 8 * width].reshape(8, seqs, piece)
+    mine = lax.dynamic_index_in_dim(mats, rank, 1, False)
+    fc_vec = lax.dynamic_index_in_dim(summed[8 * width :].reshape(seqs, -1), rank, 0, False)
+    return (
+        output,
+        input_grad,
+        qkv_weight_grad,
+        out_weight_grad,
+        fc_weight_grad,
+        proj_weight_grad,
+        mine[0],
+        mine[1],
+        mine[2:4],
+        mine[4],
+        mine[5],
+        mine[6],
+        fc_vec,
+        mine[7],
+    )
+
+
 def solution(mesh):
     placed = (
         P("dp", "seq", None),
@@ -371,8 +889,9 @@
         P("seq"),
         P("dp", "seq", None),
     )
+    fast = mesh.shape["seq"] == 4
     return jax.shard_map(
-        local,
+        local_fast if fast else local,
         mesh=mesh,
         in_specs=placed,
         out_specs=(

time: 2970 us -> 1190 us (0.40)
  waiting for transfers between devices: 2220 us -> 461 us
  matrix products: 479 us -> 190 us
  local copies, waits for them, and re-layouts: 64.3 us -> 215 us
  Pallas kernels: 0 us -> 65.9 us
  other arithmetic: 93.2 us -> 131 us
    all_gather x11 -> x3, waiting for transfers between devices: 1130 us -> 67.2 us  [the longest x1 67.2 us: local_fast(): lax.all_gather(first, ('dp', 'seq'), axis=0)]
    unnamed x32 -> x9, waiting for transfers between devices: 792 us -> 0.12 us
    dot_general x36 -> x12, matrix products: 479 us -> 190 us  [mm(): lax.dot_general(left, right, (contract, ((), ())), preferred_element_type...]
    ppermute x0 -> x20, waiting for transfers between devices: none -> 139 us  [the longest x8 139 us: swap_y(): return lax.ppermute(value, 'seq', [(i, i ^ 2) for i in range(count)])]
    reduce_scatter x5 -> x1, waiting for transfers between devices: 304 us -> 214 us  [local_fast(): lax.psum_scatter(send.reshape(dps * seqs * (qs + os), width), ('dp', 'seq...]
    pallas_call x0 -> x2, Pallas kernels: none -> 65.9 us  [the longest x1 38.4 us: attend_back_fast(): pl.pallas_call(functools.partial(attend_back_kernel, chunk, count, 2), ou...]
    slice x5 -> x28, local copies, waits for them, and re-layouts: 2.93 us -> 66.4 us  [the longest x6 35 us: cut(): return lax.slice_in_dim(value, a, b, axis=axis)]
    concatenate x1 -> x8, local copies, waits for them, and re-layouts: 0.08 us -> 59.9 us  [the longest x2 47.4 us: local_fast(): jnp.concatenate([both_cores(qkv_grad_core[i * wide:(i + 1) * wide], other...]
  transfers between devices with their start and end apart: 24 -> 31, of which waited for: 18 -> 9; matrix products, arithmetic and copies ran while one was open for 17% -> 40% of each run, Pallas kernels for 0% -> 6%
where the time goes in v1:
time: 1190 us; the launch traced here: 1180 us
  waiting for transfers between devices  461 us (39%)
  local copies, waits for them, and re-layouts  215 us (18%)
  matrix products  190 us (16%)
  other arithmetic  131 us (11%)
  blocking collectives  68.8 us (6%)
  Pallas kernels  65.9 us (6%)
  starting transfers between devices  29.2 us (2%)
  between operations  16.3 us (1%)
    reduce_scatter x1, waiting for transfers between devices, local_fast(): lax.psum_scatter(send.reshape(dps * seqs * (qs + os), width), ('dp', 'seq...  214 us
    dot_general x12, matrix products, mm(): lax.dot_general(left, right, (contract, ((), ())), preferred_element_type...  190 us
    ppermute x8, waiting for transfers between devices, swap_y(): return lax.ppermute(value, 'seq', [(i, i ^ 2) for i in range(count)])  139 us
    all_gather x1, waiting for transfers between devices, local_fast(): lax.all_gather(first, ('dp', 'seq'), axis=0)  67.2 us
    unnamed x1, blocking collectives  52.6 us
    concatenate x2, local copies, waits for them, and re-layouts, local_fast(): jnp.concatenate([both_cores(qkv_grad_core[i * wide:(i + 1) * wide], other...  47.4 us
    all_to_all x3, waiting for transfers between devices, spread(): lax.all_to_all(value.reshape(rows, seqs, -1).transpose(1, 0, 2), 'seq', 0...  41.4 us
    pallas_call x1, Pallas kernels, attend_back_fast(): pl.pallas_call(functools.partial(attend_back_kernel, chunk, count, 2), ou...  38.4 us
  transfers between devices with their start and end apart: 31, of which 9 were waited for; matrix products, arithmetic and copies ran while one was open for 40% of the time, Pallas kernels for 6%

profile of v1, /device:TPU:0, one launch (start us, length us, event | category | flops | bytes accessed | tf_op | source)
XLA Modules:
  0.0 1178.6 jit_solution(693163047224203206)
XLA Ops:
  12.2 16.2 %all_to_all.25 = bf16[4,208,400]{1,2,0:T(8,128)(2,1)S(1)} all-to-all(bf16[4,208,400]{1,2,0:T(8,128)(2,1)S(1)} %maximum_maximum_fusion), channel_id=1, replica_groups=mesh['dp'=8,'seq'=4] {'seq'}, dimensions={0} | all-to-all | bytes 1331200 | tf_op jit(solution)/shard_map/all_to_all | solution.py:675
  45.6 52.6 %all-reduce.18 = bf16[19200]{0:T(1024)(128)(2,1)S(1)} all-reduce(bf16[19200]{0:T(1024)(128)(2,1)S(1)} %dynamic-update-slice), channel_id=2, replica_groups=mesh['dp'=8,'seq'=4] {'seq'}, use_global_device_ids=true, to_apply=%add.18 | all-reduce | flops 19200 | bytes 76800
  107.7 67.2 %all-gather.5.cloned.1.call-done = bf16[32,208,1600]{2,1,0:T(8,128)(2,1)} async-done(((bf16[1,208,1600]{2,1,0:T(8,128)(2,1)}), bf16[32,208,1600]{2,1,0:T(8,128)(2,1)}) %all-gather.5.cloned.1.call-update) | async-done | bytes 21299216 | tf_op jit(solution)/shard_map/all_gather | solution.py:679
  205.2 17.2 %add_convert_fusion = bf16[1024,2688]{1,0:T(8,128)(2,1)} fusion(f32[2688]{0:T(1024)S(1)} %pad_maximum_fusion.22, bf16[896,1600]{1,0:T(8,128)(2,1)} %get-tuple-element.52, bf16[896,1600]{1,0:T(8,128)(2,1)} %get-tuple-element.53, bf16[896,1600]{1,0:T(8,128)(2,1)} %get-tuple-element.51, bf16[512,1600]{0,1:T(8,128)(2,1)} %collective-permute-done.1, ...), kind=kOutput, calls=%fused_computation.16 | convolution fusion | flops 8845901824 | bytes 17394176 | tf_op jit(solution)/shard_map/dot_general | solution.py:367
  227.7 27.5 %attend.1 = (bf16[1024,896]{1,0:T(8,128)(2,1)}, f32[56,1024]{1,0:T(8,128)}) custom-call(s32[8]{0:T(128)} %select_reduce_fusion.pos_ref, s32[14]{0:T(128)} %fusion.34.keep_ref, bf16[1024,896]{1,0:T(8,128)(2,1)} %get-tuple-element.80.q_ref, bf16[1024,896]{1,0:T(8,128)(2,1)} %get-tuple-element.79.k_ref, bf16[1024,896]{1,0:T(8,128)(2,1)} %get-tuple-element.78.v_ref), custom_call_target="tpu_custom_call" | custom-call | flops 3758096384 | bytes 7340032 | tf_op jit(solution)/shard_map/attend/pallas_call | solution.py:525
  273.7 15.8 %collective-permute-done.9 = bf16[256,1600]{0,1:T(8,128)(2,1)S(1)} collective-permute-done((bf16[256,1600]{0,1:T(8,128)(2,1)}, bf16[256,1600]{0,1:T(8,128)(2,1)S(1)}, u32[]{:S(2)}, u32[]{:S(2)}) %collective-permute-start.9) | collective-permute-done | bytes 819232 | tf_op jit(solution)/shard_map/ppermute | solution.py:611
  298.3 31.6 %collective-permute-done.11 = bf16[512,1600]{0,1:T(8,128)(2,1)} collective-permute-done((bf16[512,1600]{0,1:T(8,128)(2,1)}, bf16[512,1600]{0,1:T(8,128)(2,1)}, u32[]{:S(2)}, u32[]{:S(2)}) %collective-permute-start.11) | collective-permute-done | bytes 1638432 | tf_op jit(solution)/shard_map/ppermute | solution.py:611
  330.5 33.1 %collective-permute-done.4 = bf16[512,1600]{0,1:T(8,128)(2,1)} collective-permute-done((bf16[512,1600]{0,1:T(8,128)(2,1)}, bf16[512,1600]{0,1:T(8,128)(2,1)}, u32[]{:S(2)}, u32[]{:S(2)}) %collective-permute-start.4) | collective-permute-done | bytes 1638432 | tf_op jit(solution)/shard_map/ppermute | solution.py:611
  371.7 19.0 %fusion.30 = f32[2048,1600]{0,1:T(8,128)} fusion(bf16[1600,1600]{1,0:T(8,128)(2,1)} %all-gather.7.cloned.1.call-done, bf16[512,1600]{0,1:T(8,128)(2,1)} %collective-permute-done.5, bf16[512,1600]{0,1:T(8,128)(2,1)} %collective-permute-done.4, bf16[512,1600]{0,1:T(8,128)(2,1)} %collective-permute-done.3, bf16[512,1600]{0,1:T(8,128)(2,1)} %add_convert_fusion.2), kind=kOutput, calls=%fused_computation.111 | convolution fusion | flops 10511974400 | bytes 24780800 | tf_op jit(solution)/shard_map/dot_general | solution.py:367
  390.7 30.1 %convert_reduce_fusion = (f32[1600]{0:T(1024)S(1)}, bf16[2048,1600]{0,1:T(8,128)(2,1)}, bf16[2048,1600]{0,1:T(8,128)(2,1)}) fusion(f32[2048,1600]{0,1:T(8,128)} %fusion.30, f32[1600]{0:T(1024)S(1)} %reshape.334, bf16[2048,1600]{0,1:T(8,128)(2,1)} %constant_dynamic-update-slice_fusion, bf16[1600,1600]{1,0:T(8,128)(2,1)} %all-gather.9.cloned.1.call-done), kind=kOutput, calls=%fused_computation.13 | convolution fusion | flops 10567677952 | bytes 37900800 | tf_op jit(solution)/shard_map/dot_general | solution.py:367
  420.8 17.3 %convolution_convert_fusion.1 = bf16[1600,1600]{1,0:T(8,128)(2,1)} fusion(bf16[2048,1600]{0,1:T(8,128)(2,1)} %constant_dynamic-update-slice_fusion, bf16[2048,1600]{0,1:T(8,128)(2,1)} %get-tuple-element.57), kind=kOutput, calls=%fused_computation.18 | convolution fusion | flops 10488320000 | bytes 18227200 | tf_op jit(solution)/shard_map/dot_general | solution.py:367
  438.2 19.0 %fusion.67 = (bf16[2048,1600]{0,1:T(8,128)(2,1)S(1)}, f32[2048,1600]{0,1:T(8,128)}) fusion(bf16[2048,1600]{0,1:T(8,128)(2,1)} %get-tuple-element.33, bf16[1600,1600]{1,0:T(8,128)(2,1)} %all-gather.7.cloned.1.call-done), kind=kOutput, calls=%fused_computation.224 | convolution fusion | flops 10489036800 | bytes 31334400 | tf_op jit(solution)/shard_map/dot_general | solution.py:367
  458.6 17.8 %fusion.68 = (bf16[2048,1600]{0,1:T(8,128)(2,1)S(1)}, f32[2048,1600]{0,1:T(8,128)}) fusion(bf16[1600,1600]{1,0:T(8,128)(2,1)S(1)} %bitcast.223, bf16[2048,1600]{0,1:T(8,128)(2,1)} %get-tuple-element.57), kind=kOutput, calls=%fused_computation.225 | convolution fusion | flops 10489036800 | bytes 31334400 | tf_op jit(solution)/shard_map/dot_general | solution.py:367
  504.3 28.1 %collective-permute-done.14 = bf16[512,1600]{0,1:T(8,128)(2,1)} collective-permute-done((bf16[512,1600]{0,1:T(8,128)(2,1)}, bf16[512,1600]{0,1:T(8,128)(2,1)}, u32[]{:S(2)}, u32[]{:S(2)}) %collective-permute-start.14) | collective-permute-done | bytes 1638432 | tf_op jit(solution)/shard_map/ppermute | solution.py:611
  536.7 30.4 %collective-permute-done.7 = bf16[512,1600]{0,1:T(8,128)(2,1)} collective-permute-done((bf16[512,1600]{0,1:T(8,128)(2,1)}, bf16[512,1600]{0,1:T(8,128)(2,1)}, u32[]{:S(2)}, u32[]{:S(2)}) %collective-permute-start.7) | collective-permute-done | bytes 1638432 | tf_op jit(solution)/shard_map/ppermute | solution.py:611
  573.5 18.1 %convolution_convert_fusion.2 = bf16[1600,1600]{1,0:T(8,128)(2,1)} fusion(bf16[2048,1600]{0,1:T(8,128)(2,1)S(1)} %bitcast.225, bf16[512,1600]{0,1:T(8,128)(2,1)} %collective-permute-done.5, bf16[512,1600]{0,1:T(8,128)(2,1)} %collective-permute-done.4, bf16[512,1600]{0,1:T(8,128)(2,1)} %collective-permute-done.3, bf16[512,1600]{0,1:T(8,128)(2,1)} %add_convert_fusion.2), kind=kOutput, calls=%fused_computation.19 | convolution fusion | flops 10514534400 | bytes 18227200 | tf_op jit(solution)/shard_map/dot_general | solution.py:367
  601.3 38.4 %attend_back.1 = (bf16[1024,896]{1,0:T(8,128)(2,1)}, bf16[1024,896]{1,0:T(8,128)(2,1)}, bf16[1024,896]{1,0:T(8,128)(2,1)}) custom-call(s32[8]{0:T(128)} %select_reduce_fusion.pos_ref, s32[14]{0:T(128)} %fusion.34.keep_ref, bf16[1024,896]{1,0:T(8,128)(2,1)} %get-tuple-element.80.q_ref, bf16[1024,896]{1,0:T(8,128)(2,1)} %get-tuple-element.79.k_ref, ...), custom_call_target="tpu_custom_call" | custom-call | flops 9395240960 | bytes 14680064 | tf_op jit(solution)/shard_map/attend_back/pallas_call | solution.py:553
  642.7 16.4 %convolution_convert_fusion = bf16[2688,1600]{0,1:T(8,128)(2,1)} fusion(bf16[1024,2688]{1,0:T(8,128)(2,1)S(1)} %constant_dynamic-update-slice_fusion.5, bf16[512,1600]{0,1:T(8,128)(2,1)} %collective-permute-done.1, bf16[512,1600]{0,1:T(8,128)(2,1)} %fusion.15), kind=kOutput, calls=%fused_computation.15 | convolution fusion | flops 8818892800 | bytes 17383424 | tf_op jit(solution)/shard_map/dot_general | solution.py:367
  666.1 17.0 %fusion.13 = f32[1024,1600]{0,1:T(8,128)} fusion(bf16[1024,2688]{1,0:T(8,128)(2,1)} %copy-done.39, bf16[896,1600]{1,0:T(8,128)(2,1)} %get-tuple-element.52, bf16[896,1600]{1,0:T(8,128)(2,1)} %get-tuple-element.53, bf16[896,1600]{1,0:T(8,128)(2,1)S(1)} %copy-done.32), kind=kOutput, calls=%fused_computation.59 | convolution fusion | flops 8833843200 | bytes 20660224 | tf_op jit(solution)/shard_map/dot_general | solution.py:367
  759.5 25.4 %concatenate.200 = bf16[4800,1600]{0,1:T(8,128)(2,1)} concatenate(bf16[1600,1600]{0,1:T(8,128)(2,1)} %get-tuple-element.124, bf16[1600,1600]{0,1:T(8,128)(2,1)} %get-tuple-element.125, bf16[1600,1600]{0,1:T(8,128)(2,1)} %maximum_select_fusion.2), dimensions={0} | concatenate | bytes 30720000 | tf_op jit(solution)/shard_map/concatenate | solution.py:795
  784.9 22.0 %copy.91 = bf16[4800,1600]{1,0:T(8,128)(2,1)} copy(bf16[4800,1600]{0,1:T(8,128)(2,1)} %concatenate.200) | data formatting | bytes 30720000 | tf_op jit(solution)/shard_map/concatenate | solution.py:795
  821.9 16.2 %pad_maximum_fusion = bf16[8,4,208,1600]{3,2,0,1:T(8,128)(2,1)} fusion(bf16[8,4,56,1600]{3,2,0,1:T(8,128)(2,1)} %maximum_bitcast_fusion.1, bf16[8,4,152,1600]{3,2,0,1:T(8,128)(2,1)} %maximum_bitcast_fusion), kind=kLoop, calls=%fused_computation | loop fusion | flops 42598400 | bytes 42598400 | tf_op jit(solution)/shard_map/concatenate | solution.py:806
  881.1 40.6 %all-to-all-done.4 = bf16[4,200,400]{2,1,0:T(8,128)(2,1)S(1)} async-done(((bf16[4,200,400]{2,1,0:T(8,128)(2,1)}), bf16[4,200,400]{2,1,0:T(8,128)(2,1)S(1)}, u32[]{:S(2)}, u32[]{:S(2)}) %all-to-all-start.4) | async-done | bytes 640032 | tf_op jit(solution)/shard_map/all_to_all | solution.py:821
  931.8 213.7 %reduce-scatter.8.cloned.1.call-done = bf16[208,1600]{1,0:T(8,128)(2,1)} async-done(((bf16[6656,1600]{1,0:T(8,128)(2,1)}), bf16[208,1600]{1,0:T(8,128)(2,1)}) %reduce-scatter.8.cloned.1.call-update) | async-done | bytes 665616 | tf_op jit(solution)/shard_map/reduce_scatter | solution.py:815
  (381 shorter events, 331.6 us)
Async XLA Ops:
  7.2 167.6 %all-gather.5.cloned.1.call-start = ((), (), s32[]{:S(2)}) async-start(), calls=%async_computation.8 | async-start | bytes 22843392 | tf_op jit(solution)/shard_map/all_gather | solution.py:679
  35.5 68.3 %all-to-all-start.1 = ((bf16[4,400,400]{1,2,0:T(8,128)(2,1)}), bf16[4,400,400]{1,2,0:T(8,128)(2,1)S(1)}, u32[]{:S(2)}, u32[]{:S(2)}) async-start(bf16[4,400,400]{1,2,0:T(8,128)(2,1)} %copy.88), calls=%async_computation.1 | async-start | bytes 3276800 | tf_op jit(solution)/shard_map/all_to_all | solution.py:689
  39.2 332.5 %all-gather.7.cloned.1.call-start = ((), (), s32[]{:S(2)}) async-start(), calls=%async_computation.9 | async-start | bytes 5990400 | tf_op jit(solution)/shard_map/all_gather | solution.py:691
  41.9 59.1 %collective-permute-start = (bf16[256,1600]{0,1:T(8,128)(2,1)}, bf16[256,1600]{0,1:T(8,128)(2,1)S(1)}, u32[]{:S(2)}, u32[]{:S(2)}) collective-permute-start(bf16[256,1600]{0,1:T(8,128)(2,1)} %get-tuple-element.93), channel_id=1, source_target_pairs={{0,2},{1,3},{2,0},{3,1},{4,6},{5,7},{6,4},{7,5},{8,10},{9,11},{10,... | collective-permute-start | bytes 2457608 | tf_op jit(solution)/shard_map/ppermute | solution.py:611
  103.7 101.5 %collective-permute-start.1 = (bf16[512,1600]{0,1:T(8,128)(2,1)}, bf16[512,1600]{0,1:T(8,128)(2,1)}, u32[]{:S(2)}, u32[]{:S(2)}) collective-permute-start(bf16[512,1600]{0,1:T(8,128)(2,1)} %fusion.15), channel_id=1, source_target_pairs={{0,1},{1,0},{2,3},{3,2},{4,5},{5,4},{6,7},{7,6},{8,9},{9,8},{10,11... | collective-permute-start | bytes 4915208 | tf_op jit(solution)/shard_map/ppermute | solution.py:606
  107.6 283.1 %all-gather.9.cloned.1.call-start = ((), (), s32[]{:S(2)}) async-start(), calls=%async_computation.10 | async-start | bytes 5990400 | tf_op jit(solution)/shard_map/all_gather | solution.py:692
  271.2 594.8 %reduce-scatter.12.cloned.1.call-start = ((), (), s32[]{:S(2)}) async-start(), calls=%async_computation.14 | async-start | bytes 5990400
  290.9 39.0 %collective-permute-start.11 = (bf16[512,1600]{0,1:T(8,128)(2,1)}, bf16[512,1600]{0,1:T(8,128)(2,1)}, u32[]{:S(2)}, u32[]{:S(2)}) collective-permute-start(bf16[512,1600]{0,1:T(8,128)(2,1)} %pad_maximum_fusion.19), channel_id=1, source_target_pairs={{0,2},{1,3},{2,0},{3,1},{4,6},{5,7},{6,4},{7,5},{8,10},{9,11},{10,... | collective-permute-start | bytes 4915208 | tf_op jit(solution)/shard_map/ppermute | solution.py:611
  297.5 66.0 %collective-permute-start.4 = (bf16[512,1600]{0,1:T(8,128)(2,1)}, bf16[512,1600]{0,1:T(8,128)(2,1)}, u32[]{:S(2)}, u32[]{:S(2)}) collective-permute-start(bf16[512,1600]{0,1:T(8,128)(2,1)} %add_convert_fusion.2), channel_id=1, source_target_pairs={{0,2},{1,3},{2,0},{3,1},{4,6},{5,7},{6,4},{7,5},{8,10},{9,11},{10,... | collective-permute-start | bytes 4915208 | tf_op jit(solution)/shard_map/ppermute | solution.py:611
  298.3 66.5 %collective-permute-start.10 = (bf16[512,1600]{0,1:T(8,128)(2,1)}, bf16[512,1600]{0,1:T(8,128)(2,1)}, u32[]{:S(2)}, u32[]{:S(2)}) collective-permute-start(bf16[512,1600]{0,1:T(8,128)(2,1)} %pad_maximum_fusion.19), channel_id=1, source_target_pairs={{0,1},{1,0},{2,3},{3,2},{4,5},{5,4},{6,7},{7,6},{8,9},{9,8},{10,11... | collective-permute-start | bytes 4915208 | tf_op jit(solution)/shard_map/ppermute | solution.py:606
  329.9 40.4 %collective-permute-start.12 = (bf16[512,1600]{0,1:T(8,128)(2,1)}, bf16[512,1600]{0,1:T(8,128)(2,1)S(1)}, u32[]{:S(2)}, u32[]{:S(2)}) collective-permute-start(bf16[512,1600]{0,1:T(8,128)(2,1)} %collective-permute-done.11), channel_id=1, source_target_pairs={{0,1},{1,0},{2,3},{3,2},{4,5},{5,4},{6,7},{7,6},{8,9},{9,8},{10,11... | collective-permute-start | bytes 4915208 | tf_op jit(solution)/shard_map/ppermute | solution.py:606
  329.9 41.8 %collective-permute-start.3 = (bf16[512,1600]{0,1:T(8,128)(2,1)}, bf16[512,1600]{0,1:T(8,128)(2,1)}, u32[]{:S(2)}, u32[]{:S(2)}) collective-permute-start(bf16[512,1600]{0,1:T(8,128)(2,1)} %add_convert_fusion.2), channel_id=1, source_target_pairs={{0,1},{1,0},{2,3},{3,2},{4,5},{5,4},{6,7},{7,6},{8,9},{9,8},{10,11... | collective-permute-start | bytes 4915208 | tf_op jit(solution)/shard_map/ppermute | solution.py:606
  438.2 438.7 %reduce-scatter.10.cloned.1.call-start = ((), (), s32[]{:S(2)}) async-start(), calls=%async_computation.13 | async-start | bytes 5990400
  458.0 30.5 %collective-permute-start.13 = (bf16[1024,1600]{0,1:T(8,128)(2,1)S(1)}, bf16[1024,1600]{0,1:T(8,128)(2,1)}, u32[]{:S(2)}, u32[]{:S(2)}) collective-permute-start(bf16[1024,1600]{0,1:T(8,128)(2,1)S(1)} %pad_maximum_fusion.9), channel_id=1, source_target_pairs={{0,1},{1,0},{2,3},{3,2},{4,5},{5,4},{6,7},{7,6},{8,9},{9,8},{10,11... | collective-permute-start | bytes 9830408 | tf_op jit(solution)/shard_map/ppermute | solution.py:606
  493.4 38.9 %collective-permute-start.14 = (bf16[512,1600]{0,1:T(8,128)(2,1)}, bf16[512,1600]{0,1:T(8,128)(2,1)}, u32[]{:S(2)}, u32[]{:S(2)}) collective-permute-start(bf16[512,1600]{0,1:T(8,128)(2,1)} %slice.738), channel_id=1, source_target_pairs={{0,2},{1,3},{2,0},{3,1},{4,6},{5,7},{6,4},{7,5},{8,10},{9,11},{10,... | collective-permute-start | bytes 4915208 | tf_op jit(solution)/shard_map/ppermute | solution.py:611
  503.0 64.0 %collective-permute-start.7 = (bf16[512,1600]{0,1:T(8,128)(2,1)}, bf16[512,1600]{0,1:T(8,128)(2,1)}, u32[]{:S(2)}, u32[]{:S(2)}) collective-permute-start(bf16[512,1600]{0,1:T(8,128)(2,1)} %slice.739), channel_id=1, source_target_pairs={{0,2},{1,3},{2,0},{3,1},{4,6},{5,7},{6,4},{7,5},{8,10},{9,11},{10,... | collective-permute-start | bytes 4915208 | tf_op jit(solution)/shard_map/ppermute | solution.py:611
  591.7 336.4 %all-reduce.23.cloned.1.call-start = ((), (), s32[]{:S(2)}) async-start(), calls=%async_computation.12 | async-start | bytes 155648 | tf_op jit(solution)/shard_map/psum | solution.py:852
  659.1 68.1 %collective-permute-start.18 = (bf16[2688,1600]{0,1:T(8,128)(2,1)}, bf16[2688,1600]{0,1:T(8,128)(2,1)}, u32[]{:S(2)}, u32[]{:S(2)}) collective-permute-start(bf16[2688,1600]{0,1:T(8,128)(2,1)} %convolution_convert_fusion), channel_id=1, source_target_pairs={{0,1},{1,0},{2,3},{3,2},{4,5},{5,4},{6,7},{7,6},{8,9},{9,8},{10,11... | collective-permute-start | bytes 25804808 | tf_op jit(solution)/shard_map/ppermute | solution.py:606
  665.8 46.9 %collective-permute-start.19 = (bf16[1600,896]{1,0:T(8,128)(2,1)}, bf16[1600,896]{1,0:T(8,128)(2,1)}, u32[]{:S(2)}, u32[]{:S(2)}) collective-permute-start(bf16[1600,896]{1,0:T(8,128)(2,1)} %convolution_convert_fusion.3), channel_id=1, source_target_pairs={{0,1},{1,0},{2,3},{3,2},{4,5},{5,4},{6,7},{7,6},{8,9},{9,8},{10,11... | collective-permute-start | bytes 8601608 | tf_op jit(solution)/shard_map/ppermute | solution.py:606
  712.6 432.9 %reduce-scatter.8.cloned.1.call-start = ((), (), s32[]{:S(2)}) async-start(), calls=%async_computation.11 | async-start | bytes 22843392 | tf_op jit(solution)/shard_map/reduce_scatter | solution.py:815
  860.0 65.2 %collective-permute-start.8 = (bf16[256,1600]{0,1:T(8,128)(2,1)}, bf16[256,1600]{0,1:T(8,128)(2,1)}, u32[]{:S(2)}, u32[]{:S(2)}) collective-permute-start(bf16[256,1600]{0,1:T(8,128)(2,1)} %get-tuple-element.89), channel_id=1, source_target_pairs={{0,2},{1,3},{2,0},{3,1},{4,6},{5,7},{6,4},{7,5},{8,10},{9,11},{10,... | collective-permute-start | bytes 2457608 | tf_op jit(solution)/shard_map/ppermute | solution.py:611
  870.4 51.3 %all-to-all-start.4 = ((bf16[4,200,400]{2,1,0:T(8,128)(2,1)}), bf16[4,200,400]{2,1,0:T(8,128)(2,1)S(1)}, u32[]{:S(2)}, u32[]{:S(2)}) async-start(bf16[4,200,400]{2,1,0:T(8,128)(2,1)} %bitcast.177), calls=%async_computation.5 | async-start | bytes 1638400 | tf_op jit(solution)/shard_map/all_to_all | solution.py:821
  874.9 277.9 %collective-permute-start.17 = (bf16[256,1600]{0,1:T(8,128)(2,1)}, bf16[256,1600]{0,1:T(8,128)(2,1)}, u32[]{:S(2)}, u32[]{:S(2)}) collective-permute-start(bf16[256,1600]{0,1:T(8,128)(2,1)} %get-tuple-element.87), channel_id=1, source_target_pairs={{0,2},{1,3},{2,0},{3,1},{4,6},{5,7},{6,4},{7,5},{8,10},{9,11},{10,... | collective-permute-start | bytes 2457608 | tf_op jit(solution)/shard_map/ppermute | solution.py:611
  921.7 226.0 %all-to-all-start.3 = ((bf16[4,200,400]{2,1,0:T(8,128)(2,1)}), bf16[4,200,400]{2,1,0:T(8,128)(2,1)S(1)}, u32[]{:S(2)}, u32[]{:S(2)}) async-start(bf16[4,200,400]{2,1,0:T(8,128)(2,1)} %bitcast.201), calls=%async_computation.4 | async-start | bytes 1638400 | tf_op jit(solution)/shard_map/all_to_all | solution.py:821
  (84 other events, 1788.9 us)
Sparse Core Ops, SparseCore 0:
  29.6 145.1 all-gather.4
  177.0 85.4 all-gather.6
  271.4 84.6 all-gather.8
  438.3 121.5 reduce-scatter.11
  591.8 121.7 reduce-scatter.9
  719.6 117.9 all-reduce.22
  857.3 288.1 reduce-scatter.7
